TPU v7x, 256 devices: a whole 4x4x8 slice. The times are simulated.
256 devices in a mesh: pb: 64 (over x, z, core), ka: 4 (over y).
Axes of the slice: x: 4, y: 4, z: 8, core: 2. Of those that a mesh axis runs over, the one named last changes fastest.
Arguments:
- valence: float32 [1664, 64, 1024], P('pb', 'ka'), may hold values from -6 to 6
- conduction: bfloat16 [1664, 196, 1024], P('pb', None, 'ka'), may hold values from -0.0024414062 to 0.0024414062
- screened: float32 [64, 1024, 1024], P('pb'), may hold values from -1 to 3, as said below
- momentum: int32 [1664, 1], P('pb'), may hold values from 0 to 63; in each aligned block of 26 rows (0 to 25, 26 to 51, ...) at most 2 rows name the same one
- kpairs: int32 [1664, 2], P('pb'), may hold values from 0 to 63
- kpoint_slot: int32 [64], replicated, may hold values from 0 to 63, each once
- trial_blocks: float32 [64, 14336], P('pb', 'ka'), may hold values from -6 to 6
Outputs:
- response: float32 [64, 14336], P('pb', 'ka')
Inputs may be any that keep to these rules, and one draw needn't show every extreme that they name: Among the k-pairs of one index of pb (rows i * 26 to (i + 1) * 26 - 1), at most 2 share a momentum transfer. `kpoint_slot`: each row number appears once. `screened`: each matrix is symmetric.
All inputs are finite; a program needn't handle non-finite values.
Results may differ from a plain program's by a relative error of at most 0.0003.
Values sent between devices are 32-bit elements; how exact they have to be, the bound alone decides.
No kernel may reach another device: no remote copies, remote signals or barrier semaphores. Data moves between devices by JAX's collectives and lax.ppermute only.
A program may use at most 128 MiB of HBM per device.

v0:
```python
import jax
import jax.numpy as jnp
from jax import lax
from jax.sharding import PartitionSpec as P

VB = 8
CB = 14


def local(valence, conduction, screened, momentum, kpairs, kpoint_slot, trial_blocks):
    highest = lax.Precision.HIGHEST
    pair_dev = valence.shape[0]
    owners = lax.axis_size("pb")
    capacity = max(2, 2 * pair_dev // owners)
    slot_count = owners * capacity
    target = momentum[:, 0]
    indices = jnp.arange(pair_dev, dtype=jnp.int32)
    earlier = (target[:, None] == target[None, :]) & (indices[None, :] < indices[:, None])
    position = target * capacity + jnp.sum(earlier.astype(jnp.int32), axis=1)
    matches = position[None, :] == jnp.arange(slot_count, dtype=jnp.int32)[:, None]
    source = jnp.sum(jnp.where(matches, indices[None, :], 0), axis=1)
    filled = jnp.any(matches, axis=1)
    outgoing = jnp.where(filled[:, None, None], jnp.take(valence, source, axis=0), 0.0)
    outgoing = outgoing.reshape(owners, capacity, valence.shape[1], valence.shape[2])
    matrix = screened[0]
    product = jnp.einsum(
        "scrg,gh->scrh",
        lax.all_to_all(outgoing, "pb", split_axis=0, concat_axis=0, tiled=True),
        matrix,
        precision=highest,
        preferred_element_type=jnp.float32,
    )
    returned = lax.all_to_all(
        lax.all_to_all(product, "pb", split_axis=0, concat_axis=0, tiled=True),
        "ka",
        split_axis=3,
        concat_axis=2,
        tiled=True,
    )
    by_slot = returned.reshape(slot_count, returned.shape[2], returned.shape[3])
    columns = jnp.take(by_slot, position, axis=0)
    conduct_wide = conduction.astype(jnp.float32)
    partial_kernel = jnp.einsum(
        "prg,pbg->prb", columns, conduct_wide, precision=highest, preferred_element_type=jnp.float32
    )
    kernel = lax.psum(partial_kernel, "ka")
    gathered = lax.all_gather(trial_blocks, "pb", axis=0, tiled=True)
    kpoint_count = gathered.shape[0]
    local_trials = gathered.shape[1] // (VB * CB)
    blocks = gathered.reshape(kpoint_count, local_trials, VB, CB)
    slot_near = jnp.take(kpoint_slot, kpairs[:, 0])
    slot_far = jnp.take(kpoint_slot, kpairs[:, 1])
    near_trials = jnp.take(blocks, slot_near, axis=0)
    far_trials = jnp.take(blocks, slot_far, axis=0)
    kernel_blocks = kernel.reshape(pair_dev, VB, VB, CB, CB)
    direct = jnp.einsum("pvwcd,pnwd->pnvc", kernel_blocks, far_trials, precision=highest)
    mirror = jnp.einsum("pvwcd,pnvc->pnwd", kernel_blocks, near_trials, precision=highest)
    kpoint_rows = jnp.arange(kpoint_count, dtype=jnp.int32)[:, None]
    onehot_near = (slot_near[None, :] == kpoint_rows).astype(jnp.float32)
    onehot_far = (slot_far[None, :] == kpoint_rows).astype(jnp.float32)
    summed = jnp.dot(
        onehot_near,
        direct.reshape(pair_dev, -1),
        precision=highest,
        preferred_element_type=jnp.float32,
    )
    summed = summed + jnp.dot(
        onehot_far,
        mirror.reshape(pair_dev, -1),
        precision=highest,
        preferred_element_type=jnp.float32,
    )
    return lax.psum_scatter(summed, "pb", scatter_dimension=0, tiled=True)


def solution(mesh):
    return jax.shard_map(
        local,
        mesh=mesh,
        in_specs=(
            P("pb", "ka", None),
            P("pb", None, "ka"),
            P("pb", None, None),
            P("pb", None),
            P("pb", None),
            P(),
            P("pb", "ka"),
        ),
        out_specs=P("pb", "ka"),
        check_vma=False,
    )
```

profile of v0, /device:TPU:8, one launch (start us, length us, event | category | flops | bytes accessed | tf_op | source)
XLA Modules:
  0.0 1163.5 jit_solution(17893508544063465319)
XLA Ops:
  8.7 5.8 gather_fusion
  18.5 198.0 %all_to_all.25 = f32[64,2,16,1024]{3,2,1,0:T(8,128)S(1)} all-to-all(f32[64,2,16,1024]{3,2,1,0:T(8,128)S(1)} %select_select_fusion), channel_id=1, replica_groups=mesh['pb'=64,'ka'=4] {'pb'}, dimensions={0} | all-to-all | bytes 16777216 | tf_op jit(solution)/shard_map/all_to_all | solution.py:28
  216.4 27.7 %fusion = f32[64,2,16,1024]{3,2,1,0:T(8,128)S(1)} fusion(f32[64,2,16,1024]{3,2,1,0:T(8,128)S(1)} %all_to_all.25, f32[1,1024,1024]{2,1,0:T(8,128)S(1)} %copy-done.5), kind=kOutput, calls=%fused_computation.8 | convolution fusion | flops 25769803776 | bytes 20971520 | tf_op jit(solution)/shard_map/scrg,gh->scrh/dot_general | solution.py:26
  244.1 192.1 %all_to_all.26 = f32[64,2,16,1024]{3,2,1,0:T(8,128)} all-to-all(f32[64,2,16,1024]{3,2,1,0:T(8,128)S(1)} %fusion), channel_id=1, replica_groups=mesh['pb'=64,'ka'=4] {'pb'}, dimensions={0} | all-to-all | bytes 16777216 | tf_op jit(solution)/shard_map/all_to_all | solution.py:34
  436.2 16.3 %copy.61 = f32[64,2,16,1024]{0,2,1,3:T(8,128)} copy(f32[64,2,16,1024]{3,2,1,0:T(8,128)} %all_to_all.26) | data formatting | bytes 16777216 | tf_op jit(solution)/shard_map/all_to_all | solution.py:34
  452.5 14.3 %reshape.142 = f32[4,1,524288]{2,1,0:T(1,128)} reshape(f32[1024,2,16,64]{3,2,1,0:T(8,128)} %bitcast.68) | data formatting | bytes 16777216
  466.8 6.2 all-to-all-start.2
  473.0 92.9 %all-to-all-done.2 = f32[4,1,524288]{2,1,0:T(1,128)} async-done(((f32[4,1,524288]{2,1,0:T(1,128)}), f32[4,1,524288]{2,1,0:T(1,128)}, u32[]{:S(2)}, u32[]{:S(2)}) %all-to-all-start.2) | async-done | bytes 8388640 | tf_op jit(solution)/shard_map/all_to_all | solution.py:33
  566.5 30.1 %reduce = f32[4,524288]{1,0:T(4,128)} reduce(f32[4,1,524288]{2,1,0:T(1,128)} %all-to-all-done.2, f32[]{:T(128)} %broadcast.181), dimensions={1}, to_apply=%all_to_all.19.reduce_sub_computation | reduce | bytes 16777220 | tf_op jit(solution)/shard_map/all_to_all | solution.py:33
  596.6 16.8 %reshape.143 = f32[1024,2,16,64]{3,2,1,0:T(8,128)} reshape(f32[4,524288]{1,0:T(4,128)} %reduce) | data formatting | bytes 16777216
  613.4 14.4 %copy.75 = f32[64,2,16,4,256]{4,3,2,1,0:T(4,128)} copy(f32[64,2,16,4,256]{0,2,1,4,3:T(8,128)} %bitcast.69) | data formatting | bytes 16777216 | tf_op jit(solution)/shard_map/all_to_all | solution.py:33
  627.8 8.6 copy.63
  636.4 5.3 gather_fusion.1
  641.7 5.3 fusion.2
  647.0 5.8 copy.64
  652.8 14.5 %copy.65 = f32[26,8,8,14,14]{3,2,4,1,0:T(8,128)} copy(f32[26,8,8,14,14]{0,2,1,4,3:T(8,128)} %bitcast.72) | data formatting | bytes 2609152 | tf_op jit(solution)/shard_map/reshape | solution.py:55
  669.4 52.6 %all-gather = f32[64,1,3584]{2,1,0:T(1,128)} all-gather(f32[1,1,3584]{2,1,0:T(1,128)S(1)} %bitcast.74), channel_id=1, replica_groups=mesh['pb'=64,'ka'=4] {'pb'}, dimensions={0}, use_global_device_ids=true | all-gather | bytes 931840 | tf_op jit(solution)/shard_map/all_gather | solution.py:47
  728.7 5.5 copy.60
  741.9 142.4 %all-reduce.4.cloned.1.call-done = f32[26,8,8,14,14]{3,2,4,1,0:T(8,128)} async-done(((f32[26,8,8,14,14]{3,2,4,1,0:T(8,128)}), f32[26,8,8,14,14]{3,2,4,1,0:T(8,128)}) %all-reduce.4.cloned.1.call-update) | async-done | bytes 1304592 | tf_op jit(solution)/shard_map/psum | solution.py:46
  884.3 16.3 %copy.68 = f32[26,8,8,14,14]{4,1,3,2,0:T(8,128)} copy(f32[26,8,8,14,14]{3,2,4,1,0:T(8,128)} %all-reduce.4.cloned.1.call-done) | data formatting | bytes 2609152 | tf_op jit(solution)/shard_map/psum | solution.py:46
  900.7 22.8 %convolution_bitcast_fusion = f32[26,32,8,14]{1,3,2,0:T(8,128)} fusion(f32[26,8,8,14,14]{4,1,3,2,0:T(8,128)} %copy.68, f32[26,32,8,14]{1,2,3,0:T(8,128)} %gather_fusion.5, pred[26]{0:T(512)(128)(4,1)S(1)} %get-tuple-element.6), kind=kOutput, calls=%fused_computation.12 | convolution fusion | flops 125332480 | bytes 2050074 | tf_op jit(solution)/shard_map/pvwcd,pnvc->pnwd/dot_general | solution.py:57
  931.2 23.0 %convolution_bitcast_fusion.1 = f32[26,32,8,14]{1,3,2,0:T(8,128)} fusion(f32[26,8,8,14,14]{3,2,4,1,0:T(8,128)} %all-reduce.4.cloned.1.call-done, f32[26,32,8,14]{1,2,3,0:T(8,128)} %gather_fusion.4, pred[26]{0:T(512)(128)(4,1)S(1)} %get-tuple-element.13), kind=kOutput, calls=%fused_computation.13 | convolution fusion | flops 125332480 | bytes 2050074 | tf_op jit(solution)/shard_map/pvwcd,pnwd->pnvc/dot_general | solution.py:56
  957.9 4.6 reshape.71
  966.2 188.0 %all-reduce.6.cloned.1.call-done = f32[64,3584]{1,0:T(8,128)} async-done(((f32[64,3584]{1,0:T(8,128)}), f32[64,3584]{1,0:T(8,128)}) %all-reduce.6.cloned.1.call-update) | async-done | bytes 917520
  (51 shorter events, 40.4 us)
Async XLA Ops:
  6.5 635.1 %copy-start = (bf16[26,196,256]{2,1,0:T(8,128)(2,1)S(1)}, bf16[26,196,256]{2,1,0:T(8,128)(2,1)}, u32[]{:S(2)}) copy-start(bf16[26,196,256]{2,1,0:T(8,128)(2,1)} %param.12) | copy-start | bytes 7827460
  18.4 198.0 %copy-start.5 = (f32[1,1024,1024]{2,1,0:T(8,128)S(1)}, f32[1,1024,1024]{2,1,0:T(8,128)}, u32[]{:S(2)}) copy-start(f32[1,1024,1024]{2,1,0:T(8,128)} %param.13) | copy-start | bytes 12582916
  466.8 6.2 copy-start.4
  466.8 99.1 %all-to-all-start.2 = ((f32[4,1,524288]{2,1,0:T(1,128)}), f32[4,1,524288]{2,1,0:T(1,128)}, u32[]{:S(2)}, u32[]{:S(2)}) async-start(f32[4,1,524288]{2,1,0:T(1,128)} %reshape.142), calls=%async_computation.2 | async-start | bytes 16777216 | tf_op jit(solution)/shard_map/all_to_all | solution.py:33
  473.0 411.3 %all-reduce.4.cloned.1.call-start = ((), (), s32[]{:S(2)}) async-start(), calls=%async_computation.3 | async-start | bytes 23855104 | tf_op jit(solution)/shard_map/psum | solution.py:46
  667.3 0.7 copy-start.3
  667.3 0.7 copy-start.1
  667.3 2.1 copy-start.2
  667.3 486.9 %all-reduce.6.cloned.1.call-start = ((), (), s32[]{:S(2)}) async-start(), calls=%async_computation.4 | async-start | bytes 1835008
  957.9 7.6 copy-start.6
Sparse Core Ops, SparseCore 0:
  667.4 216.8 all-reduce.3
  965.7 188.5 all-reduce.5
where the time goes:
time: 1170 us; the launch traced here: 1160 us
  blocking collectives  443 us (38%)
  waiting for transfers between devices  423 us (36%)
  local copies, waits for them, and re-layouts  160 us (14%)
  matrix products  81.8 us (7%)
  other arithmetic  36 us (3%)
  between operations  13.8 us (1%)
    all_to_all x1, blocking collectives, local(): lax.all_to_all(outgoing, 'pb', split_axis=0, concat_axis=0, tiled=True)  198 us
    all_to_all x1, blocking collectives, local(): lax.all_to_all(product, 'pb', split_axis=0, concat_axis=0, tiled=True)  192 us
    unnamed x3, waiting for transfers between devices  188 us
    psum x1, waiting for transfers between devices, local(): kernel = lax.psum(partial_kernel, 'ka')  142 us
    all_to_all x1, waiting for transfers between devices, local(): lax.all_to_all(lax.all_to_all(product, 'pb', split_axis=0, concat_axis=0,...  92.9 us
    all_gather x1, blocking collectives, local(): gathered = lax.all_gather(trial_blocks, 'pb', axis=0, tiled=True)  52.6 us
    unnamed x18, local copies, waits for them, and re-layouts  34.6 us
    all_to_all x1, other arithmetic, local(): lax.all_to_all(lax.all_to_all(product, 'pb', split_axis=0, concat_axis=0,...  30.1 us
  transfers between devices with their start and end apart: 3, of which 3 were waited for; matrix products, arithmetic and copies ran while one was open for 2% of the time, Pallas kernels for 0%

commit v1 on v0

--- a/solution.py
+++ b/solution.py
@@ -43,7 +43,9 @@
     partial_kernel = jnp.einsum(
         "prg,pbg->prb", columns, conduct_wide, precision=highest, preferred_element_type=jnp.float32
     )
-    kernel = lax.psum(partial_kernel, "ka")
+    kernel = partial_kernel
+    for hop in (1, 2):
+        kernel = kernel + lax.ppermute(kernel, "ka", [(dev, dev ^ hop) for dev in range(4)])
     gathered = lax.all_gather(trial_blocks, "pb", axis=0, tiled=True)
     kpoint_count = gathered.shape[0]
     local_trials = gathered.shape[1] // (VB * CB)

time: 1170 us -> 1070 us (0.915)
  waiting for transfers between devices: 423 us -> 313 us
    psum x1 -> x0, waiting for transfers between devices: 142 us -> none  [local(): kernel = lax.psum(partial_kernel, 'ka')]
    ppermute x0 -> x2, waiting for transfers between devices: none -> 37 us  [local(): lax.ppermute(kernel, 'ka', [(dev, dev ^ hop) for dev in range(4)])]
    psum x1 -> x0, local copies, waits for them, and re-layouts: 16.3 us -> none  [local(): kernel = lax.psum(partial_kernel, 'ka')]
    reshape x1 -> x2, local copies, waits for them, and re-layouts: 14.5 us -> 29.1 us  [local(): kernel_blocks = kernel.reshape(pair_dev, VB, VB, CB, CB)]
    unnamed x3 -> x2, waiting for transfers between devices: 188 us -> 183 us
  transfers between devices with their start and end apart: 3 -> 4, of which waited for: 3 -> 3; matrix products, arithmetic and copies ran while one was open for 2% -> 2% of each run, Pallas kernels for 0% -> 0%
where the time goes in v1:
time: 1070 us; the launch traced here: 1060 us
  blocking collectives  444 us (41%)
  waiting for transfers between devices  313 us (29%)
  local copies, waits for them, and re-layouts  157 us (15%)
  matrix products  81.5 us (8%)
  other arithmetic  41.1 us (4%)
  between operations  13.8 us (1%)
    all_to_all x1, blocking collectives, local(): lax.all_to_all(outgoing, 'pb', split_axis=0, concat_axis=0, tiled=True)  198 us
    all_to_all x1, blocking collectives, local(): lax.all_to_all(product, 'pb', split_axis=0, concat_axis=0, tiled=True)  192 us
    unnamed x2, waiting for transfers between devices  183 us
    all_to_all x1, waiting for transfers between devices, local(): lax.all_to_all(lax.all_to_all(product, 'pb', split_axis=0, concat_axis=0,...  92.9 us
    all_gather x1, blocking collectives, local(): gathered = lax.all_gather(trial_blocks, 'pb', axis=0, tiled=True)  54.2 us
    ppermute x2, waiting for transfers between devices, local(): lax.ppermute(kernel, 'ka', [(dev, dev ^ hop) for dev in range(4)])  37 us
    unnamed x18, local copies, waits for them, and re-layouts  34 us
    all_to_all x1, other arithmetic, local(): lax.all_to_all(lax.all_to_all(product, 'pb', split_axis=0, concat_axis=0,...  30.1 us
  transfers between devices with their start and end apart: 4, of which 3 were waited for; matrix products, arithmetic and copies ran while one was open for 2% of the time, Pallas kernels for 0%

profile of v1, /device:TPU:8, one launch (start us, length us, event | category | flops | bytes accessed | tf_op | source)
XLA Modules:
  0.0 1059.6 jit_solution(545944887493288051)
XLA Ops:
  8.7 5.8 gather_fusion
  18.5 198.0 %all_to_all.25 = f32[64,2,16,1024]{3,2,1,0:T(8,128)S(1)} all-to-all(f32[64,2,16,1024]{3,2,1,0:T(8,128)S(1)} %select_select_fusion), channel_id=1, replica_groups=mesh['pb'=64,'ka'=4] {'pb'}, dimensions={0} | all-to-all | bytes 16777216 | tf_op jit(solution)/shard_map/all_to_all | solution.py:28
  216.4 27.7 %fusion = f32[64,2,16,1024]{3,2,1,0:T(8,128)S(1)} fusion(f32[64,2,16,1024]{3,2,1,0:T(8,128)S(1)} %all_to_all.25, f32[1,1024,1024]{2,1,0:T(8,128)S(1)} %copy-done.5), kind=kOutput, calls=%fused_computation.8 | convolution fusion | flops 25769803776 | bytes 20971520 | tf_op jit(solution)/shard_map/scrg,gh->scrh/dot_general | solution.py:26
  244.1 192.1 %all_to_all.26 = f32[64,2,16,1024]{3,2,1,0:T(8,128)} all-to-all(f32[64,2,16,1024]{3,2,1,0:T(8,128)S(1)} %fusion), channel_id=1, replica_groups=mesh['pb'=64,'ka'=4] {'pb'}, dimensions={0} | all-to-all | bytes 16777216 | tf_op jit(solution)/shard_map/all_to_all | solution.py:34
  436.2 16.3 %copy.61 = f32[64,2,16,1024]{0,2,1,3:T(8,128)} copy(f32[64,2,16,1024]{3,2,1,0:T(8,128)} %all_to_all.26) | data formatting | bytes 16777216 | tf_op jit(solution)/shard_map/all_to_all | solution.py:34
  452.5 14.3 %reshape.142 = f32[4,1,524288]{2,1,0:T(1,128)} reshape(f32[1024,2,16,64]{3,2,1,0:T(8,128)} %bitcast.68) | data formatting | bytes 16777216
  466.8 6.2 all-to-all-start.2
  473.0 92.9 %all-to-all-done.2 = f32[4,1,524288]{2,1,0:T(1,128)} async-done(((f32[4,1,524288]{2,1,0:T(1,128)}), f32[4,1,524288]{2,1,0:T(1,128)}, u32[]{:S(2)}, u32[]{:S(2)}) %all-to-all-start.2) | async-done | bytes 8388640 | tf_op jit(solution)/shard_map/all_to_all | solution.py:33
  566.5 30.1 %reduce = f32[4,524288]{1,0:T(4,128)} reduce(f32[4,1,524288]{2,1,0:T(1,128)} %all-to-all-done.2, f32[]{:T(128)} %broadcast.181), dimensions={1}, to_apply=%all_to_all.19.reduce_sub_computation | reduce | bytes 16777220 | tf_op jit(solution)/shard_map/all_to_all | solution.py:33
  596.6 16.8 %reshape.143 = f32[1024,2,16,64]{3,2,1,0:T(8,128)} reshape(f32[4,524288]{1,0:T(4,128)} %reduce) | data formatting | bytes 16777216
  613.4 14.4 %copy.75 = f32[64,2,16,4,256]{4,3,2,1,0:T(4,128)} copy(f32[64,2,16,4,256]{0,2,1,4,3:T(8,128)} %bitcast.69) | data formatting | bytes 16777216 | tf_op jit(solution)/shard_map/all_to_all | solution.py:33
  627.8 8.6 copy.63
  636.4 5.3 gather_fusion.1
  641.7 4.1 fusion.2
  647.3 37.0 %collective-permute-done = f32[26,64,196]{2,1,0:T(8,128)S(1)} collective-permute-done((f32[26,64,196]{2,1,0:T(8,128)S(1)}, f32[26,64,196]{2,1,0:T(8,128)S(1)}, u32[]{:S(2)}, u32[]{:S(2)}) %collective-permute-start) | collective-permute-done | bytes 1304608 | tf_op jit(solution)/shard_map/ppermute | solution.py:48
  688.6 54.2 %all-gather = f32[64,1,3584]{2,1,0:T(1,128)} all-gather(f32[1,1,3584]{2,1,0:T(1,128)S(1)} %bitcast.75), channel_id=1, replica_groups=mesh['pb'=64,'ka'=4] {'pb'}, dimensions={0}, use_global_device_ids=true | all-gather | bytes 931840 | tf_op jit(solution)/shard_map/all_gather | solution.py:49
  742.8 4.0 copy.59
  749.5 5.5 copy.60
  766.1 5.7 copy.64
  771.9 14.5 %copy.65 = f32[26,8,8,14,14]{3,2,4,1,0:T(8,128)} copy(f32[26,8,8,14,14]{0,2,1,4,3:T(8,128)} %bitcast.70) | data formatting | bytes 2609152 | tf_op jit(solution)/shard_map/reshape | solution.py:57
  786.4 14.6 %copy.68 = f32[26,8,8,14,14]{4,1,3,2,0:T(8,128)} copy(f32[26,8,8,14,14]{0,2,1,4,3:T(8,128)} %bitcast.71) | data formatting | bytes 2609152 | tf_op jit(solution)/shard_map/reshape | solution.py:57
  801.0 22.8 %convolution_bitcast_fusion.1 = f32[26,32,8,14]{1,3,2,0:T(8,128)} fusion(f32[26,8,8,14,14]{3,2,4,1,0:T(8,128)} %copy.65, f32[26,32,8,14]{1,2,3,0:T(8,128)} %gather_fusion.4, pred[26]{0:T(512)(128)(4,1)S(1)} %get-tuple-element.13), kind=kOutput, calls=%fused_computation.13 | convolution fusion | flops 125332480 | bytes 2050074 | tf_op jit(solution)/shard_map/pvwcd,pnwd->pnvc/dot_general | solution.py:58
  833.1 22.8 %convolution_bitcast_fusion = f32[26,32,8,14]{1,3,2,0:T(8,128)} fusion(f32[26,8,8,14,14]{4,1,3,2,0:T(8,128)} %copy.68, f32[26,32,8,14]{1,2,3,0:T(8,128)} %gather_fusion.5, pred[26]{0:T(512)(128)(4,1)S(1)} %get-tuple-element.6), kind=kOutput, calls=%fused_computation.12 | convolution fusion | flops 125332480 | bytes 2050074 | tf_op jit(solution)/shard_map/pvwcd,pnvc->pnwd/dot_general | solution.py:59
  866.9 183.4 %all-reduce.3.cloned.1.call-done = f32[64,3584]{1,0:T(8,128)} async-done(((f32[64,3584]{1,0:T(8,128)}), f32[64,3584]{1,0:T(8,128)}) %all-reduce.3.cloned.1.call-update) | async-done | bytes 917520
  (54 shorter events, 48.6 us)
Async XLA Ops:
  6.5 635.1 %copy-start = (bf16[26,196,256]{2,1,0:T(8,128)(2,1)S(1)}, bf16[26,196,256]{2,1,0:T(8,128)(2,1)}, u32[]{:S(2)}) copy-start(bf16[26,196,256]{2,1,0:T(8,128)(2,1)} %param.12) | copy-start | bytes 7827460
  18.5 198.0 %copy-start.5 = (f32[1,1024,1024]{2,1,0:T(8,128)S(1)}, f32[1,1024,1024]{2,1,0:T(8,128)}, u32[]{:S(2)}) copy-start(f32[1,1024,1024]{2,1,0:T(8,128)} %param.13) | copy-start | bytes 12582916
  466.8 6.2 copy-start.4
  466.8 99.1 %all-to-all-start.2 = ((f32[4,1,524288]{2,1,0:T(1,128)}), f32[4,1,524288]{2,1,0:T(1,128)}, u32[]{:S(2)}, u32[]{:S(2)}) async-start(f32[4,1,524288]{2,1,0:T(1,128)} %reshape.142), calls=%async_computation.2 | async-start | bytes 16777216 | tf_op jit(solution)/shard_map/all_to_all | solution.py:33
  473.0 577.3 %all-reduce.3.cloned.1.call-start = ((), (), s32[]{:S(2)}) async-start(), calls=%async_computation.3 | async-start | bytes 1835008
  645.8 41.3 %copy-start.3 = (s32[26,2]{0,1:T(2,128)S(1)}, s32[26,2]{0,1:T(2,128)}, u32[]{:S(2)}) copy-start(s32[26,2]{0,1:T(2,128)} %param.15) | copy-start | bytes 628
  645.8 41.3 %copy-start.1 = (s32[64]{0:T(128)S(1)}, s32[64]{0:T(128)}, u32[]{:S(2)}) copy-start(s32[64]{0:T(128)} %param.16) | copy-start | bytes 772
  645.9 42.7 %copy-start.2 = (f32[1,3584]{1,0:T(1,128)S(1)}, f32[1,3584]{1,0:T(1,128)}, u32[]{:S(2)}) copy-start(f32[1,3584]{1,0:T(1,128)} %param.17) | copy-start | bytes 43012
  645.9 38.5 %collective-permute-start = (f32[26,64,196]{2,1,0:T(8,128)S(1)}, f32[26,64,196]{2,1,0:T(8,128)S(1)}, u32[]{:S(2)}, u32[]{:S(2)}) collective-permute-start(f32[26,64,196]{2,1,0:T(8,128)S(1)} %fusion.2), channel_id=1, source_target_pairs={{0,1},{1,0},{2,3},{3,2},{4,5},{5,4},{6,7},{7,6},{8,9},{9,8},{10,11... | collective-permute-start | bytes 3913736 | tf_op jit(solution)/shard_map/ppermute | solution.py:48
  685.8 76.8 %collective-permute-start.1 = (f32[26,64,196]{2,1,0:T(8,128)}, f32[26,64,196]{2,1,0:T(8,128)}, u32[]{:S(2)}, u32[]{:S(2)}) collective-permute-start(f32[26,64,196]{2,1,0:T(8,128)} %add.63), channel_id=1, source_target_pairs={{0,2},{1,3},{2,0},{3,1},{4,6},{5,7},{6,4},{7,5},{8,10},{9,11},{10,... | collective-permute-start | bytes 3913736 | tf_op jit(solution)/shard_map/ppermute | solution.py:48
  859.6 6.7 copy-start.6
Sparse Core Ops, SparseCore 0:
  866.4 183.9 all-reduce.2
